TPU v7x, 32 devices: a whole 2x2x4 slice. The times are simulated.
32 devices in a mesh: row: 2 (over x), col: 16 (over z, y, core).
Axes of the slice: x: 2, y: 2, z: 4, core: 2. Of those that a mesh axis runs over, the one named last changes fastest.
Arguments:
- chol_window: bfloat16 [512, 8, 1024], P('row', None, 'col'), may hold values from -6 to 6
- pair_vectors: bfloat16 [512, 512, 1024], P('row', 'col'), may hold values from -0.1875 to 0.1875
- amplitudes: bfloat16 [512, 512, 256], P('row', 'col'), may hold values from -0.015625 to 0.015625
Outputs:
- ladder: float32 [8, 256, 512], P(None, 'col', 'row')
All inputs are finite; a program needn't handle non-finite values.
Results may differ from a plain program's by a relative error of at most 0.0029.
Values may be sent and summed in bfloat16 or wider, within the bound.
A program may use at most 320 MiB of HBM per device.

v0:
```python
import jax
import jax.numpy as jnp
from jax import lax
from jax.sharding import PartitionSpec as P


def local(chol_window, pair_vectors, amplitudes):
    window = lax.all_gather(chol_window, "col", axis=2, tiled=True)
    c_rows, width_a, chol_count = window.shape
    block_rows = pair_vectors.shape[0]
    d_cols = pair_vectors.shape[1]
    pair_count = amplitudes.shape[2]

    def ladder_term(chol_rows, vectors_flat, amplitude_block, b_rows):
        integrals = lax.dot_general(
            chol_rows.reshape(-1, chol_count),
            vectors_flat,
            (((1,), (1,)), ((), ())),
            preferred_element_type=jnp.float32,
        )
        integrals = integrals.astype(jnp.bfloat16).reshape(
            chol_rows.shape[0], width_a, b_rows, d_cols
        )
        return jnp.einsum(
            "cabd,cdn->anb", integrals, amplitude_block, preferred_element_type=jnp.float32
        )

    vectors_flat = pair_vectors.reshape(block_rows * d_cols, chol_count)
    zeros_init = jnp.zeros((width_a, pair_count, block_rows), jnp.float32)
    running = zeros_init
    segments = (
        lax.all_gather(window, "row", axis=0, tiled=True),
        lax.all_gather(amplitudes, "row", axis=0, tiled=True),
    )
    row_count = segments[0].shape[0]
    chol_blocks = segments[0].reshape(row_count // c_rows, c_rows, width_a, chol_count)
    amp_blocks = segments[1].reshape(row_count // c_rows, c_rows, d_cols, pair_count)

    def scan_step(carry, operands):
        return (carry + ladder_term(operands[0], vectors_flat, operands[1], block_rows), None)

    running, unused = lax.scan(scan_step, running, (chol_blocks, amp_blocks))
    result = lax.psum_scatter(running, "col", scatter_dimension=1, tiled=True)
    return result


def solution(mesh):
    return jax.shard_map(
        local,
        mesh=mesh,
        in_specs=(P("row", None, "col"), P("row", "col", None), P("row", "col", None)),
        out_specs=P(None, "col", "row"),
        check_vma=False,
    )
```

profile of v0, /device:TPU:13, one launch (start us, length us, event | category | flops | bytes accessed | tf_op | source)
XLA Modules:
  0.0 974.2 jit_solution(14329805057244354373)
XLA Ops:
  6.5 0.0 all-gather.6.cloned.1.call-start
  6.5 0.7 all-gather.6.cloned.1.call-update
  7.3 0.0 all-gather.8.cloned.1.call-start
  7.3 53.3 %all-gather.6.cloned.1.call-done = bf16[256,8,1024]{0,2,1:T(8,128)(2,1)} async-done(((bf16[256,8,64]{0,2,1:T(8,128)(2,1)}), bf16[256,8,1024]{0,2,1:T(8,128)(2,1)}) %all-gather.6.cloned.1.call-update) | async-done | bytes 4194320 | tf_op jit(solution)/shard_map/all_gather | solution.py:8
  60.6 0.0 all-gather.8.cloned.1.call-update
  60.6 0.0 all-gather.4.cloned.1.call-start
  60.7 0.7 all-gather.4.cloned.1.call-update
  61.4 0.0 reduce-scatter.2.cloned.1.call-start
  61.4 103.5 %all-gather.8.cloned.1.call-done = bf16[512,8,1024]{0,2,1:T(8,128)(2,1)} async-done(((bf16[256,8,1024]{0,2,1:T(8,128)(2,1)}), bf16[512,8,1024]{0,2,1:T(8,128)(2,1)}) %all-gather.8.cloned.1.call-update) | async-done | bytes 8388624 | tf_op jit(solution)/shard_map/all_gather | solution.py:32
  164.9 12.9 %copy.10 = bf16[512,8,1024]{2,1,0:T(8,128)(2,1)} copy(bf16[512,8,1024]{0,2,1:T(8,128)(2,1)} %all-gather.8.cloned.1.call-done) | data formatting | bytes 16777216 | tf_op jit(solution)/shard_map/all_gather | solution.py:32
  177.8 92.7 %all-gather.4.cloned.1.call-done = bf16[512,32,256]{2,1,0:T(8,128)(2,1)} async-done(((bf16[256,32,256]{2,1,0:T(8,128)(2,1)}), bf16[512,32,256]{2,1,0:T(8,128)(2,1)}) %all-gather.4.cloned.1.call-update) | async-done | bytes 8388624 | tf_op jit(solution)/shard_map/all_gather | solution.py:33
  270.5 637.3 %while.11 = (s32[]{:T(128)}, f32[8,256,256]{2,1,0:T(8,128)}, bf16[2,256,32,256]{3,2,1,0:T(8,128)(2,1)}, bf16[2,256,8,1024]{3,2,1,0:T(8,128)(2,1)}, bf16[8192,1024]{1,0:T(8,128)(2,1)}, /*index=5*/s32[]{:T(128)}, s32[]{:T(128)}) while((s32[]{:T(128)}, f32[8,256,256]{2,1,0:T(8,128)}, bf16[2,256,32,256]{3,2,1,0:T(8,128)(2,1)}, ...), condition=%wide.region_1.2_spmd.clone, body=%wide.region_0.1_spmd.clone.sunk | while | flops 42967498752 | bytes 264241808 | solution.py:42
  270.5 42.5 %convolution_convert_fusion.2 = bf16[2048,8192]{1,0:T(8,128)(2,1)} fusion(bf16[8192,1024]{1,0:T(8,128)(2,1)} %get-tuple-element.120, bf16[2,256,8,1024]{3,2,1,0:T(8,128)(2,1)} %get-tuple-element.119, s32[]{:T(128)} %get-tuple-element.109), kind=kOutput, calls=%fused_computation.clone.2 | convolution fusion | flops 34376515584 | bytes 54526464 | tf_op jit(solution)/shard_map/while/body/eval_jaxpr/dot_general | solution.py:15
  313.0 126.4 %reshape.24 = bf16[256,8,256,32]{3,2,1,0:T(8,128)(2,1)} reshape(bf16[2048,8192]{1,0:T(8,128)(2,1)} %convolution_convert_fusion.2) | data formatting | bytes 67108864 | tf_op jit(solution)/shard_map/while/body/eval_jaxpr/reshape | solution.py:21
  439.4 119.8 %copy.16 = bf16[256,8,256,32]{2,0,3,1:T(8,128)(2,1)} copy(bf16[256,8,256,32]{3,2,1,0:T(8,128)(2,1)} %reshape.24) | data formatting | bytes 67108864 | tf_op jit(solution)/shard_map/while/body/eval_jaxpr/reshape | solution.py:21
  559.2 4.6 constant_dynamic-slice_fusion.2
  563.8 7.7 copy.17
  571.4 0.0 copy-done
  571.4 16.3 %bitcast_add_fusion.2 = f32[8,256,256]{2,1,0:T(8,128)S(1)} fusion(f32[8,256,256]{2,1,0:T(8,128)S(1)} %copy-done, bf16[256,8,256,32]{2,0,3,1:T(8,128)(2,1)} %copy.16, bf16[1,256,32,256]{1,3,2,0:T(8,128)(2,1)} %copy.17, pred[]{:T(512)S(6)} %compare.3), kind=kOutput, calls=%fused_computation.5.clone.1 | convolution fusion | flops 8590983168 | bytes 41943040 | tf_op jit(solution)/shard_map/while/body/eval_jaxpr/cabd,cdn->anb/dot_general | solution.py:24
  587.8 0.0 copy-start.1
  587.8 1.3 copy-done.1
  589.1 42.5 %convolution_convert_fusion.2 = bf16[2048,8192]{1,0:T(8,128)(2,1)} fusion(bf16[8192,1024]{1,0:T(8,128)(2,1)} %get-tuple-element.120, bf16[2,256,8,1024]{3,2,1,0:T(8,128)(2,1)} %get-tuple-element.119, s32[]{:T(128)} %get-tuple-element.109), kind=kOutput, calls=%fused_computation.clone.2 | convolution fusion | flops 34376515584 | bytes 54526464 | tf_op jit(solution)/shard_map/while/body/eval_jaxpr/dot_general | solution.py:15
  631.6 126.4 %reshape.24 = bf16[256,8,256,32]{3,2,1,0:T(8,128)(2,1)} reshape(bf16[2048,8192]{1,0:T(8,128)(2,1)} %convolution_convert_fusion.2) | data formatting | bytes 67108864 | tf_op jit(solution)/shard_map/while/body/eval_jaxpr/reshape | solution.py:21
  758.0 119.8 %copy.16 = bf16[256,8,256,32]{2,0,3,1:T(8,128)(2,1)} copy(bf16[256,8,256,32]{3,2,1,0:T(8,128)(2,1)} %reshape.24) | data formatting | bytes 67108864 | tf_op jit(solution)/shard_map/while/body/eval_jaxpr/reshape | solution.py:21
  877.8 4.6 constant_dynamic-slice_fusion.2
  882.4 7.7 copy.17
  890.1 0.0 copy-done
  890.1 16.3 %bitcast_add_fusion.2 = f32[8,256,256]{2,1,0:T(8,128)S(1)} fusion(f32[8,256,256]{2,1,0:T(8,128)S(1)} %copy-done, bf16[256,8,256,32]{2,0,3,1:T(8,128)(2,1)} %copy.16, bf16[1,256,32,256]{1,3,2,0:T(8,128)(2,1)} %copy.17, pred[]{:T(512)S(6)} %compare.3), kind=kOutput, calls=%fused_computation.5.clone.1 | convolution fusion | flops 8590983168 | bytes 41943040 | tf_op jit(solution)/shard_map/while/body/eval_jaxpr/cabd,cdn->anb/dot_general | solution.py:24
  906.4 0.0 copy-start.1
  906.4 1.3 copy-done.1
  907.7 0.0 reduce-scatter.2.cloned.1.call-update
  907.8 59.9 %reduce-scatter.2.cloned.1.call-done = f32[8,16,256]{2,1,0:T(8,128)} async-done(((f32[8,256,256]{2,1,0:T(8,128)}), f32[8,16,256]{2,1,0:T(8,128)}) %reduce-scatter.2.cloned.1.call-update) | async-done | bytes 131088 | tf_op jit(solution)/shard_map/reduce_scatter | solution.py:43
  (3 shorter events, 0.0 us)
Async XLA Ops:
  6.5 54.1 %all-gather.6.cloned.1.call-start = ((), (), s32[]{:S(2)}) async-start(), calls=%async_computation.2 | async-start | bytes 4456448 | tf_op jit(solution)/shard_map/all_gather | solution.py:8
  7.3 157.7 %all-gather.8.cloned.1.call-start = ((), (), s32[]{:S(2)}) async-start(), calls=%async_computation.3 | async-start | bytes 12582912 | tf_op jit(solution)/shard_map/all_gather | solution.py:32
  60.6 209.9 %all-gather.4.cloned.1.call-start = ((), (), s32[]{:S(2)}) async-start(), calls=%async_computation.1 | async-start | bytes 12582912 | tf_op jit(solution)/shard_map/all_gather | solution.py:33
  61.4 906.4 %reduce-scatter.2.cloned.1.call-start = ((), (), s32[]{:S(2)}) async-start(), calls=%async_computation.4 | async-start | bytes 2228224 | tf_op jit(solution)/shard_map/reduce_scatter | solution.py:43
  563.8 7.7 copy-start
  587.8 1.3 copy-start.1
  882.4 7.7 copy-start
  906.4 1.3 copy-start.1
Sparse Core Ops, SparseCore 0:
  9.5 51.0 all-gather.5
  62.1 102.7 all-gather.7
  166.5 103.9 all-gather.3
  907.9 59.7 reduce-scatter.1
where the time goes:
time: 991 us; the launch traced here: 974 us
  local copies, waits for them, and re-layouts  532 us (54%)
  waiting for transfers between devices  311 us (31%)
  matrix products  118 us (12%)
  between operations  13.1 us (1%)
    reshape x4, local copies, waits for them, and re-layouts, ladder_term(): integrals.astype(jnp.bfloat16)  492 us
    all_gather x1, waiting for transfers between devices, local(): lax.all_gather(window, 'row', axis=0, tiled=True)  104 us
    all_gather x1, waiting for transfers between devices, local(): lax.all_gather(amplitudes, 'row', axis=0, tiled=True)  92.7 us
    dot_general x2, matrix products, ladder_term(): lax.dot_general(chol_rows.reshape(-1, chol_count), vectors_flat, (((1,),...  85 us
    reduce_scatter x1, waiting for transfers between devices, local(): result = lax.psum_scatter(running, 'col', scatter_dimension=1, tiled=True)  59.9 us
    all_gather x1, waiting for transfers between devices, local(): window = lax.all_gather(chol_window, 'col', axis=2, tiled=True)  53.3 us
    dot_general x2, matrix products, ladder_term(): jnp.einsum('cabd,cdn->anb', integrals, amplitude_block, preferred_element...  32.7 us
    dynamic_slice x4, local copies, waits for them, and re-layouts, local(): running, unused = lax.scan(scan_step, running, (chol_blocks, amp_blocks))  24.5 us
  transfers between devices with their start and end apart: 4, of which 4 were waited for; matrix products, arithmetic and copies ran while one was open for 1% of the time, Pallas kernels for 0%

commit v1 on v0

v1 whole, which is shorter than its diff:
```python
import functools

import jax
import jax.numpy as jnp
from jax import lax
from jax.experimental import pallas as pl
from jax.experimental.pallas import tpu as pltpu
from jax.sharding import PartitionSpec as P

A_GROUPS = 4
D_BLOCK = 4


def ladder_kernel(c, last, first, p_ref, w_ref, t_ref, *rest):
    if first:
        out_ref, it, acc = rest
    else:
        prev_ref, out_ref, it, acc = rest
    step = pl.program_id(0)
    d_block, b, q = p_ref.shape
    groups = w_ref.shape[1] // c
    n = t_ref.shape[2]

    @pl.when(step == 0)
    def _():
        acc[...] = jnp.zeros_like(acc) if first else prev_ref[...]

    rows = p_ref[...].reshape(d_block * b, q)
    for a in range(groups):
        term = jnp.dot(rows, w_ref[:, a * c:(a + 1) * c], preferred_element_type=jnp.float32)
        term = term.astype(jnp.bfloat16)
        for d in range(d_block):
            it[a * b:(a + 1) * b, d * c:(d + 1) * c] = term[d * b:(d + 1) * b]
    acc[...] += jnp.dot(it[...], t_ref[...].reshape(d_block * c, n), preferred_element_type=jnp.float32)

    @pl.when(step == pl.num_programs(0) - 1)
    def _():
        out_ref[...] = acc[...].T if last else acc[...]


def ladder_call(p_t, w, t, prev, last):
    d, b, q = p_t.shape
    c, n = t.shape[1], t.shape[2]
    width = w.shape[1]
    rows = width // c * b
    d_block = D_BLOCK if d % D_BLOCK == 0 else 1
    out = (n, rows) if last else (rows, n)
    whole = lambda shape: pl.BlockSpec(shape, lambda i: (0,) * len(shape))
    in_specs = [
        pl.BlockSpec((d_block, b, q), lambda i: (i, 0, 0)),
        whole((q, width)),
        pl.BlockSpec((d_block, c, n), lambda i: (i, 0, 0)),
    ]
    args = [p_t, w, t]
    if prev is not None:
        in_specs.append(whole((rows, n)))
        args.append(prev)
    flops = 2 * d * b * width * (q + n)
    return pl.pallas_call(
        functools.partial(ladder_kernel, c, last, prev is None),
        out_shape=jax.ShapeDtypeStruct(out, jnp.float32),
        grid=(d // d_block,),
        in_specs=in_specs,
        out_specs=whole(out),
        scratch_shapes=[
            pltpu.VMEM((rows, d_block * c), jnp.bfloat16),
            pltpu.VMEM((rows, n), jnp.float32),
        ],
        cost_estimate=pl.CostEstimate(flops=flops, bytes_accessed=2 * (p_t.size + w.size + t.size), transcendentals=0),
        compiler_params=pltpu.CompilerParams(vmem_limit_bytes=56 * 2**20),
    )(*args)


def local(row_count, chol_window, pair_vectors, amplitudes):
    c, width_a, q_own = chol_window.shape
    b = pair_vectors.shape[0]
    groups = A_GROUPS if width_a % A_GROUPS == 0 else 1
    per = width_a // groups

    w_own = chol_window.transpose(2, 1, 0)
    t_own = amplitudes.transpose(1, 0, 2)
    if row_count == 1:
        blocks = [(w_own, t_own)]
    elif c % 128 == 0:
        blocks = [(w_own, t_own)]
        for shift in range(1, row_count):
            pairs = [(i, (i + shift) % row_count) for i in range(row_count)]
            blocks.append((lax.ppermute(w_own, "row", pairs), lax.ppermute(t_own, "row", pairs)))
    else:
        blocks = [(
            lax.all_gather(w_own, "row", axis=2, tiled=True),
            lax.all_gather(t_own, "row", axis=1, tiled=True),
        )]
    p_t = pair_vectors.transpose(1, 0, 2)

    sums = [None] * groups
    for index, (w, t) in enumerate(blocks):
        for g in range(groups):
            piece = w[:, g * per:(g + 1) * per].reshape(q_own, -1)
            piece = lax.all_gather(piece, "col", axis=0, tiled=True)
            sums[g] = ladder_call(p_t, piece, t, sums[g], index == len(blocks) - 1)
    parts = [lax.psum_scatter(s, "col", scatter_dimension=0, tiled=True) for s in sums]
    parts = [s.reshape(s.shape[0], per, b).transpose(1, 0, 2) for s in parts]
    return jnp.concatenate(parts, axis=0)


def solution(mesh):
    return jax.shard_map(
        functools.partial(local, mesh.shape["row"]),
        mesh=mesh,
        in_specs=(P("row", None, "col"), P("row", "col", None), P("row", "col", None)),
        out_specs=P(None, "col", "row"),
        check_vma=False,
    )
```

time: 991 us -> 567 us (0.57); the launches traced: 974 us -> 562 us
  local copies, waits for them, and re-layouts: 532 us -> 34.3 us
  Pallas kernels: 0 us -> 144 us
  matrix products: 118 us -> 0 us
  waiting for transfers between devices: 311 us -> 366 us
    reshape x4 -> x12, local copies, waits for them, and re-layouts: 492 us -> 8.07 us  [the longest x8 5.03 us: local(): piece = w[:, g * per:(g + 1) * per].reshape(q_own, -1)]
    reduce_scatter x1 -> x4, waiting for transfers between devices: 59.9 us -> 213 us  [local(): lax.psum_scatter(s, 'col', scatter_dimension=0, tiled=True)]
    pallas_call x0 -> x8, Pallas kernels: none -> 144 us  [ladder_call(): pl.pallas_call(functools.partial(ladder_kernel, c, last, prev is None), o...]
    dot_general x4 -> x0, matrix products: 118 us -> none  [the longest x2 85 us: ladder_term(): lax.dot_general(chol_rows.reshape(-1, chol_count), vectors_flat, (((1,),...]
    all_gather x3 -> x8, waiting for transfers between devices: 250 us -> 147 us  [local(): piece = lax.all_gather(piece, 'col', axis=0, tiled=True)]
    unnamed x0 -> x4, local copies, waits for them, and re-layouts: none -> 26.2 us
    dynamic_slice x4 -> x0, local copies, waits for them, and re-layouts: 24.5 us -> none  [local(): running, unused = lax.scan(scan_step, running, (chol_blocks, amp_blocks))]
    all_gather x1 -> x0, local copies, waits for them, and re-layouts: 12.9 us -> none  [local(): lax.all_gather(window, 'row', axis=0, tiled=True)]
  transfers between devices with their start and end apart: 4 -> 14, of which waited for: 4 -> 13; matrix products, arithmetic and copies ran while one was open for 1% -> 6% of each run, Pallas kernels for 0% -> 26%
where the time goes in v1:
time: 567 us; the launch traced here: 562 us
  waiting for transfers between devices  366 us (65%)
  Pallas kernels  144 us (25%)
  local copies, waits for them, and re-layouts  34.3 us (6%)
  between operations  13.6 us (2%)
    reduce_scatter x4, waiting for transfers between devices, local(): lax.psum_scatter(s, 'col', scatter_dimension=0, tiled=True)  213 us
    all_gather x8, waiting for transfers between devices, local(): piece = lax.all_gather(piece, 'col', axis=0, tiled=True)  147 us
    pallas_call x8, Pallas kernels, ladder_call(): pl.pallas_call(functools.partial(ladder_kernel, c, last, prev is None), o...  144 us
    unnamed x4, local copies, waits for them, and re-layouts  26.2 us
  transfers between devices with their start and end apart: 14, of which 13 were waited for; matrix products, arithmetic and copies ran while one was open for 6% of the time, Pallas kernels for 26%

profile of v1, /device:TPU:13, one launch (start us, length us, event | category | flops | bytes accessed | tf_op | source)
XLA Modules:
  0.0 561.9 jit_solution(5836186717374671365)
XLA Ops:
  6.5 1.0 slice_bitcast_fusion.6
  8.2 0.6 copy.25
  9.7 0.6 copy.29
  10.4 1.3 collective-permute-start
  11.7 6.2 %collective-permute-done = bf16[64,8,256]{2,0,1:T(8,128)(2,1)S(1)} collective-permute-done((bf16[64,8,256]{2,0,1:T(8,128)(2,1)}, bf16[64,8,256]{2,0,1:T(8,128)(2,1)S(1)}, u32[]{:S(2)}, u32[]{:S(2)}) %collective-permute-start) | collective-permute-done | bytes 262176 | tf_op jit(solution)/shard_map/ppermute | solution.py:88
  20.0 6.6 %copy.37 = bf16[256,32,256]{2,0,1:T(8,128)(2,1)} copy(bf16[256,32,256]{2,1,0:T(8,128)(2,1)} %param.5) | data formatting | bytes 8388608 | tf_op args[2]
  26.6 1.2 collective-permute-start.1
  27.8 18.7 %copy.36 = bf16[256,32,1024]{2,0,1:T(8,128)(2,1)} copy(bf16[256,32,1024]{2,1,0:T(8,128)(2,1)} %param.4) | data formatting | bytes 33554432 | tf_op args[1]
  47.5 17.9 %shard_map.37.rest_0_ = f32[512,256]{1,0:T(8,128)} custom-call(bf16[32,256,1024]{2,1,0:T(8,128)(2,1)} %bitcast.59, bf16[1024,512]{1,0:T(8,128)(2,1)} %all-gather.11.cloned.1.call-done.w_ref, bf16[32,256,256]{2,1,0:T(8,128)(2,1)} %bitcast.50.t_ref), custom_call_target="tpu_custom_call" | custom-call | flops 10737418240 | bytes 22020096 | tf_op jit(solution)/shard_map/pallas_call | solution.py:59
  65.4 21.2 %all-gather.15.cloned.1.call-done.w_ref = bf16[1024,512]{1,0:T(8,128)(2,1)} async-done(((bf16[64,512]{1,0:T(8,128)(2,1)}), bf16[1024,512]{1,0:T(8,128)(2,1)}) %all-gather.15.cloned.1.call-update) | async-done | bytes 1048592 | tf_op jit(solution)/shard_map/all_gather | solution.py:100
  86.6 17.9 %shard_map.39.rest_0_ = f32[512,256]{1,0:T(8,128)} custom-call(bf16[32,256,1024]{2,1,0:T(8,128)(2,1)} %bitcast.60, bf16[1024,512]{1,0:T(8,128)(2,1)} %all-gather.15.cloned.1.call-done.w_ref, bf16[32,256,256]{2,1,0:T(8,128)(2,1)} %bitcast.50.t_ref), custom_call_target="tpu_custom_call" | custom-call | flops 10737418240 | bytes 22020096 | tf_op jit(solution)/shard_map/pallas_call | solution.py:59
  104.4 21.2 %all-gather.19.cloned.1.call-done.w_ref = bf16[1024,512]{1,0:T(8,128)(2,1)} async-done(((bf16[64,512]{1,0:T(8,128)(2,1)}), bf16[1024,512]{1,0:T(8,128)(2,1)}) %all-gather.19.cloned.1.call-update) | async-done | bytes 1048592 | tf_op jit(solution)/shard_map/all_gather | solution.py:100
  125.6 17.9 %shard_map.41.rest_0_ = f32[512,256]{1,0:T(8,128)} custom-call(bf16[32,256,1024]{2,1,0:T(8,128)(2,1)} %bitcast.61, bf16[1024,512]{1,0:T(8,128)(2,1)} %all-gather.19.cloned.1.call-done.w_ref, bf16[32,256,256]{2,1,0:T(8,128)(2,1)} %bitcast.50.t_ref), custom_call_target="tpu_custom_call" | custom-call | flops 10737418240 | bytes 22020096 | tf_op jit(solution)/shard_map/pallas_call | solution.py:59
  143.5 21.0 %all-gather.23.cloned.1.call-done.w_ref = bf16[1024,512]{1,0:T(8,128)(2,1)} async-done(((bf16[64,512]{1,0:T(8,128)(2,1)}), bf16[1024,512]{1,0:T(8,128)(2,1)}) %all-gather.23.cloned.1.call-update) | async-done | bytes 1048592 | tf_op jit(solution)/shard_map/all_gather | solution.py:100
  164.4 17.9 %shard_map.43.rest_0_ = f32[512,256]{1,0:T(8,128)} custom-call(bf16[32,256,1024]{2,1,0:T(8,128)(2,1)} %bitcast.62, bf16[1024,512]{1,0:T(8,128)(2,1)} %all-gather.23.cloned.1.call-done.w_ref, bf16[32,256,256]{2,1,0:T(8,128)(2,1)} %bitcast.50.t_ref), custom_call_target="tpu_custom_call" | custom-call | flops 10737418240 | bytes 22020096 | tf_op jit(solution)/shard_map/pallas_call | solution.py:59
  182.3 21.0 %all-gather.9.cloned.1.call-done.w_ref = bf16[1024,512]{1,0:T(8,128)(2,1)} async-done(((bf16[64,512]{1,0:T(8,128)(2,1)}), bf16[1024,512]{1,0:T(8,128)(2,1)}) %all-gather.9.cloned.1.call-update) | async-done | bytes 1048592 | tf_op jit(solution)/shard_map/all_gather | solution.py:100
  203.3 18.3 %shard_map.38 = f32[256,512]{1,0:T(8,128)} custom-call(bf16[32,256,1024]{2,1,0:T(8,128)(2,1)} %bitcast.63, bf16[1024,512]{1,0:T(8,128)(2,1)} %all-gather.9.cloned.1.call-done.w_ref, bf16[32,256,256]{2,1,0:T(8,128)(2,1)} %collective-permute-done.1.t_ref, f32[512,256]{1,0:T(8,128)} %shard_map.37.rest_0_), custom_call_target="tpu_custom_call" | custom-call | flops 10737418240 | bytes 22020096 | tf_op jit(solution)/shard_map/pallas_call | solution.py:59
  221.7 20.5 %all-gather.13.cloned.1.call-done.w_ref = bf16[1024,512]{1,0:T(8,128)(2,1)} async-done(((bf16[64,512]{1,0:T(8,128)(2,1)}), bf16[1024,512]{1,0:T(8,128)(2,1)}) %all-gather.13.cloned.1.call-update) | async-done | bytes 1048592 | tf_op jit(solution)/shard_map/all_gather | solution.py:100
  242.2 18.1 %shard_map.40 = f32[256,512]{1,0:T(8,128)} custom-call(bf16[32,256,1024]{2,1,0:T(8,128)(2,1)} %bitcast.64, bf16[1024,512]{1,0:T(8,128)(2,1)} %all-gather.13.cloned.1.call-done.w_ref, bf16[32,256,256]{2,1,0:T(8,128)(2,1)} %collective-permute-done.1.t_ref, f32[512,256]{1,0:T(8,128)} %shard_map.39.rest_0_), custom_call_target="tpu_custom_call" | custom-call | flops 10737418240 | bytes 22020096 | tf_op jit(solution)/shard_map/pallas_call | solution.py:59
  260.4 20.8 %all-gather.17.cloned.1.call-done.w_ref = bf16[1024,512]{1,0:T(8,128)(2,1)} async-done(((bf16[64,512]{1,0:T(8,128)(2,1)}), bf16[1024,512]{1,0:T(8,128)(2,1)}) %all-gather.17.cloned.1.call-update) | async-done | bytes 1048592 | tf_op jit(solution)/shard_map/all_gather | solution.py:100
  281.3 18.2 %shard_map.42 = f32[256,512]{1,0:T(8,128)} custom-call(bf16[32,256,1024]{2,1,0:T(8,128)(2,1)} %bitcast.65, bf16[1024,512]{1,0:T(8,128)(2,1)} %all-gather.17.cloned.1.call-done.w_ref, bf16[32,256,256]{2,1,0:T(8,128)(2,1)} %collective-permute-done.1.t_ref, f32[512,256]{1,0:T(8,128)} %shard_map.41.rest_0_), custom_call_target="tpu_custom_call" | custom-call | flops 10737418240 | bytes 22020096 | tf_op jit(solution)/shard_map/pallas_call | solution.py:59
  299.5 20.8 %all-gather.21.cloned.1.call-done.w_ref = bf16[1024,512]{1,0:T(8,128)(2,1)} async-done(((bf16[64,512]{1,0:T(8,128)(2,1)}), bf16[1024,512]{1,0:T(8,128)(2,1)}) %all-gather.21.cloned.1.call-update) | async-done | bytes 1048592 | tf_op jit(solution)/shard_map/all_gather | solution.py:100
  320.3 18.2 %shard_map.44 = f32[256,512]{1,0:T(8,128)} custom-call(bf16[32,256,1024]{2,1,0:T(8,128)(2,1)} %bitcast.66, bf16[1024,512]{1,0:T(8,128)(2,1)} %all-gather.21.cloned.1.call-done.w_ref, bf16[32,256,256]{2,1,0:T(8,128)(2,1)} %collective-permute-done.1.t_ref, f32[512,256]{1,0:T(8,128)} %shard_map.43.rest_0_), custom_call_target="tpu_custom_call" | custom-call | flops 10737418240 | bytes 22020096 | tf_op jit(solution)/shard_map/pallas_call | solution.py:59
  338.4 39.1 %reduce-scatter.5.cloned.1.call-done = f32[16,512]{1,0:T(8,128)} async-done(((f32[256,512]{1,0:T(8,128)}), f32[16,512]{1,0:T(8,128)}) %reduce-scatter.5.cloned.1.call-update) | async-done | bytes 32784 | tf_op jit(solution)/shard_map/reduce_scatter | solution.py:102
  377.6 0.8 copy.41
  378.3 57.9 %reduce-scatter.7.cloned.1.call-done = f32[16,512]{1,0:T(8,128)} async-done(((f32[256,512]{1,0:T(8,128)}), f32[16,512]{1,0:T(8,128)}) %reduce-scatter.7.cloned.1.call-update) | async-done | bytes 32784 | tf_op jit(solution)/shard_map/reduce_scatter | solution.py:102
  436.2 0.8 copy.40
  437.0 58.0 %reduce-scatter.9.cloned.1.call-done = f32[16,512]{1,0:T(8,128)} async-done(((f32[256,512]{1,0:T(8,128)}), f32[16,512]{1,0:T(8,128)}) %reduce-scatter.9.cloned.1.call-update) | async-done | bytes 32784 | tf_op jit(solution)/shard_map/reduce_scatter | solution.py:102
  495.0 0.8 copy.39
  495.8 57.9 %reduce-scatter.11.cloned.1.call-done = f32[16,512]{1,0:T(8,128)} async-done(((f32[256,512]{1,0:T(8,128)}), f32[16,512]{1,0:T(8,128)}) %reduce-scatter.11.cloned.1.call-update) | async-done | bytes 32784 | tf_op jit(solution)/shard_map/reduce_scatter | solution.py:102
  553.6 0.8 copy.38
  554.4 0.7 pad_maximum_fusion
  (33 shorter events, 4.9 us)
Async XLA Ops:
  6.5 41.0 %all-gather.11.cloned.1.call-start = ((), (), s32[]{:S(2)}) async-start(), calls=%async_computation.5 | async-start | bytes 1114112 | tf_op jit(solution)/shard_map/all_gather | solution.py:100
  8.1 78.4 %all-gather.15.cloned.1.call-start = ((), (), s32[]{:S(2)}) async-start(), calls=%async_computation.8 | async-start | bytes 1114112 | tf_op jit(solution)/shard_map/all_gather | solution.py:100
  8.9 116.7 %all-gather.19.cloned.1.call-start = ((), (), s32[]{:S(2)}) async-start(), calls=%async_computation.11 | async-start | bytes 1114112 | tf_op jit(solution)/shard_map/all_gather | solution.py:100
  9.6 154.8 %all-gather.23.cloned.1.call-start = ((), (), s32[]{:S(2)}) async-start(), calls=%async_computation.14 | async-start | bytes 1114112 | tf_op jit(solution)/shard_map/all_gather | solution.py:100
  10.3 193.0 %all-gather.9.cloned.1.call-start = ((), (), s32[]{:S(2)}) async-start(), calls=%async_computation.4 | async-start | bytes 1114112 | tf_op jit(solution)/shard_map/all_gather | solution.py:100
  10.4 7.5 %collective-permute-start = (bf16[64,8,256]{2,0,1:T(8,128)(2,1)}, bf16[64,8,256]{2,0,1:T(8,128)(2,1)S(1)}, u32[]{:S(2)}, u32[]{:S(2)}) collective-permute-start(bf16[64,8,256]{2,0,1:T(8,128)(2,1)} %bitcast.68), channel_id=1, source_target_pairs={{0,16},{16,0},{1,17},{17,1},{2,18},{18,2},{3,19},{19,3},{4,20},{20... | collective-permute-start | bytes 786440 | tf_op jit(solution)/shard_map/ppermute | solution.py:88
  18.5 223.7 %all-gather.13.cloned.1.call-start = ((), (), s32[]{:S(2)}) async-start(), calls=%async_computation.7 | async-start | bytes 1114112 | tf_op jit(solution)/shard_map/all_gather | solution.py:100
  19.2 262.0 %all-gather.17.cloned.1.call-start = ((), (), s32[]{:S(2)}) async-start(), calls=%async_computation.10 | async-start | bytes 1114112 | tf_op jit(solution)/shard_map/all_gather | solution.py:100
  20.0 300.3 %all-gather.21.cloned.1.call-start = ((), (), s32[]{:S(2)}) async-start(), calls=%async_computation.13 | async-start | bytes 1114112 | tf_op jit(solution)/shard_map/all_gather | solution.py:100
  26.6 176.7 %collective-permute-start.1 = (bf16[32,256,256]{2,1,0:T(8,128)(2,1)}, bf16[32,256,256]{2,1,0:T(8,128)(2,1)}, u32[]{:S(2)}, u32[]{:S(2)}) collective-permute-start(bf16[32,256,256]{2,1,0:T(8,128)(2,1)} %bitcast.50.t_ref), channel_id=1, source_target_pairs={{0,16},{16,0},{1,17},{17,1},{2,18},{18,2},{3,19},{19,3},{4,20},{20... | collective-permute-start | bytes 12582920 | tf_op jit(solution)/shard_map/ppermute | solution.py:88
  47.2 330.4 %reduce-scatter.5.cloned.1.call-start = ((), (), s32[]{:S(2)}) async-start(), calls=%async_computation.6 | async-start | bytes 557056 | tf_op jit(solution)/shard_map/reduce_scatter | solution.py:102
  221.6 214.6 %reduce-scatter.7.cloned.1.call-start = ((), (), s32[]{:S(2)}) async-start(), calls=%async_computation.9 | async-start | bytes 557056 | tf_op jit(solution)/shard_map/reduce_scatter | solution.py:102
  260.4 234.6 %reduce-scatter.9.cloned.1.call-start = ((), (), s32[]{:S(2)}) async-start(), calls=%async_computation.12 | async-start | bytes 557056 | tf_op jit(solution)/shard_map/reduce_scatter | solution.py:102
  299.4 254.2 %reduce-scatter.11.cloned.1.call-start = ((), (), s32[]{:S(2)}) async-start(), calls=%async_computation.15 | async-start | bytes 557056 | tf_op jit(solution)/shard_map/reduce_scatter | solution.py:102
Sparse Core Ops, SparseCore 0:
  9.5 38.0 all-gather.10
  49.7 36.8 all-gather.14
  88.7 36.8 all-gather.18
  127.6 36.7 all-gather.22
  166.5 36.8 all-gather.8
  205.3 36.8 all-gather.12
  244.4 36.8 all-gather.16
  283.4 36.7 all-gather.20
  323.8 53.7 reduce-scatter.4
  381.0 55.2 reduce-scatter.6
  439.8 55.1 reduce-scatter.8
  498.4 55.1 reduce-scatter.10

commit v2 on v1

--- a/solution.py
+++ b/solution.py
@@ -7,7 +7,7 @@
 from jax.experimental.pallas import tpu as pltpu
 from jax.sharding import PartitionSpec as P
 
-A_GROUPS = 4
+MESH = pl.DeviceIdType.MESH
 D_BLOCK = 4
 
 
@@ -35,7 +35,7 @@
 
     @pl.when(step == pl.num_programs(0) - 1)
     def _():
-        out_ref[...] = acc[...].T if last else acc[...]
+        out_ref[...] = acc[...].T.astype(out_ref.dtype) if last else acc[...]
 
 
 def ladder_call(p_t, w, t, prev, last):
@@ -58,7 +58,7 @@
     flops = 2 * d * b * width * (q + n)
     return pl.pallas_call(
         functools.partial(ladder_kernel, c, last, prev is None),
-        out_shape=jax.ShapeDtypeStruct(out, jnp.float32),
+        out_shape=jax.ShapeDtypeStruct(out, jnp.bfloat16 if last else jnp.float32),
         grid=(d // d_block,),
         in_specs=in_specs,
         out_specs=whole(out),
@@ -67,15 +67,58 @@
             pltpu.VMEM((rows, n), jnp.float32),
         ],
         cost_estimate=pl.CostEstimate(flops=flops, bytes_accessed=2 * (p_t.size + w.size + t.size), transcendentals=0),
-        compiler_params=pltpu.CompilerParams(vmem_limit_bytes=56 * 2**20),
+        compiler_params=pltpu.CompilerParams(vmem_limit_bytes=60 * 2**20),
     )(*args)
 
 
-def local(row_count, chol_window, pair_vectors, amplitudes):
+def scatter_kernel(cols, x_ref, out_ref, held, send_sem, recv_sem):
+    me = lax.axis_index("col")
+    barrier = pltpu.get_barrier_semaphore()
+    for s in range(1, cols):
+        pl.semaphore_signal(barrier, inc=1, device_id={"col": lax.rem(me + s, cols)}, device_id_type=MESH)
+    pl.semaphore_wait(barrier, cols - 1)
+    copies = []
+    for s in range(1, cols):
+        to = lax.rem(me + s, cols)
+        copy = pltpu.make_async_remote_copy(
+            src_ref=x_ref.at[to],
+            dst_ref=held.at[s - 1],
+            send_sem=send_sem.at[s - 1],
+            recv_sem=recv_sem.at[s - 1],
+            device_id={"col": to},
+            device_id_type=MESH,
+        )
+        copy.start()
+        copies.append(copy)
+    total = x_ref[me].astype(jnp.float32)
+    for s, copy in enumerate(copies):
+        copy.wait_recv()
+        total = total + held[s].astype(jnp.float32)
+    out_ref[...] = total
+    for copy in copies:
+        copy.wait_send()
+
+
+def scatter_call(x, cols):
+    n, width = x.shape
+    piece = (n // cols, width)
+    return pl.pallas_call(
+        functools.partial(scatter_kernel, cols),
+        out_shape=jax.ShapeDtypeStruct(piece, jnp.float32),
+        in_specs=[pl.BlockSpec(memory_space=pltpu.VMEM)],
+        out_specs=pl.BlockSpec(memory_space=pltpu.VMEM),
+        scratch_shapes=[
+            pltpu.VMEM((cols - 1, *piece), x.dtype),
+            pltpu.SemaphoreType.DMA((cols - 1,)),
+            pltpu.SemaphoreType.DMA((cols - 1,)),
+        ],
+        compiler_params=pltpu.CompilerParams(collective_id=0, has_side_effects=True),
+    )(x.reshape(cols, *piece))
+
+
+def local(row_count, col_count, chol_window, pair_vectors, amplitudes):
     c, width_a, q_own = chol_window.shape
     b = pair_vectors.shape[0]
-    groups = A_GROUPS if width_a % A_GROUPS == 0 else 1
-    per = width_a // groups
 
     w_own = chol_window.transpose(2, 1, 0)
     t_own = amplitudes.transpose(1, 0, 2)
@@ -93,20 +136,17 @@
         )]
     p_t = pair_vectors.transpose(1, 0, 2)
 
-    sums = [None] * groups
+    total = None
     for index, (w, t) in enumerate(blocks):
-        for g in range(groups):
-            piece = w[:, g * per:(g + 1) * per].reshape(q_own, -1)
-            piece = lax.all_gather(piece, "col", axis=0, tiled=True)
-            sums[g] = ladder_call(p_t, piece, t, sums[g], index == len(blocks) - 1)
-    parts = [lax.psum_scatter(s, "col", scatter_dimension=0, tiled=True) for s in sums]
-    parts = [s.reshape(s.shape[0], per, b).transpose(1, 0, 2) for s in parts]
-    return jnp.concatenate(parts, axis=0)
+        w = lax.all_gather(w.reshape(q_own, -1), "col", axis=0, tiled=True)
+        total = ladder_call(p_t, w, t, total, index == len(blocks) - 1)
+    out = scatter_call(total, col_count)
+    return out.reshape(out.shape[0], width_a, b).transpose(1, 0, 2)
 
 
 def solution(mesh):
     return jax.shard_map(
-        functools.partial(local, mesh.shape["row"]),
+        functools.partial(local, mesh.shape["row"], mesh.shape["col"]),
         mesh=mesh,
         in_specs=(P("row", None, "col"), P("row", "col", None), P("row", "col", None)),
         out_specs=P(None, "col", "row"),

time: 567 us -> 204 us (0.36)
  waiting for transfers between devices: 366 us -> 27.6 us
  Pallas kernels: 144 us -> 131 us
    reduce_scatter x4 -> x0, waiting for transfers between devices: 213 us -> none  [local(): lax.psum_scatter(s, 'col', scatter_dimension=0, tiled=True)]
    all_gather x8 -> x2, waiting for transfers between devices: 147 us -> 17.6 us  [local(): w = lax.all_gather(w.reshape(q_own, -1), 'col', axis=0, tiled=True)]
    pallas_call x8 -> x2, Pallas kernels: 144 us -> 99.5 us  [ladder_call(): pl.pallas_call(functools.partial(ladder_kernel, c, last, prev is None), o...]
    pallas_call x0 -> x1, Pallas kernels: none -> 31.5 us  [scatter_call(): pl.pallas_call(functools.partial(scatter_kernel, cols), out_shape=jax.Sha...]
    unnamed x4 -> x2, local copies, waits for them, and re-layouts: 26.2 us -> 25.3 us
  transfers between devices with their start and end apart: 14 -> 4, of which waited for: 13 -> 3; matrix products, arithmetic and copies ran while one was open for 6% -> 13% of each run, Pallas kernels for 26% -> 24%
where the time goes in v2:
time: 204 us
  Pallas kernels  131 us (64%)
  local copies, waits for them, and re-layouts  29.2 us (14%)
  waiting for transfers between devices  27.6 us (14%)
  between operations  13.4 us (7%)
  starting transfers between devices  2.53 us (1%)
    pallas_call x2, Pallas kernels, ladder_call(): pl.pallas_call(functools.partial(ladder_kernel, c, last, prev is None), o...  99.5 us
    pallas_call x1, Pallas kernels, scatter_call(): pl.pallas_call(functools.partial(scatter_kernel, cols), out_shape=jax.Sha...  31.5 us
    unnamed x2, local copies, waits for them, and re-layouts  25.3 us
    all_gather x2, waiting for transfers between devices, local(): w = lax.all_gather(w.reshape(q_own, -1), 'col', axis=0, tiled=True)  17.6 us
    ppermute x1, waiting for transfers between devices, local(): lax.ppermute(w_own, 'row', pairs)  6.19 us
  transfers between devices with their start and end apart: 4, of which 3 were waited for; matrix products, arithmetic and copies ran while one was open for 13% of the time, Pallas kernels for 24%

profile of v2, /device:TPU:13, one launch (start us, length us, event | category | flops | bytes accessed | tf_op | source)
XLA Modules:
  0.0 203.8 jit_solution(5811710587797612034)
XLA Ops:
  6.5 0.0 all-gather.5.cloned.1.call-start
  6.5 1.7 copy.11
  8.2 0.0 all-gather.5.cloned.1.call-update
  8.2 0.0 all-gather.3.cloned.1.call-start
  8.3 1.3 collective-permute-start
  9.6 6.2 %collective-permute-done = bf16[64,8,256]{2,0,1:T(8,128)(2,1)S(1)} collective-permute-done((bf16[64,8,256]{2,0,1:T(8,128)(2,1)}, bf16[64,8,256]{2,0,1:T(8,128)(2,1)S(1)}, u32[]{:S(2)}, u32[]{:S(2)}) %collective-permute-start) | collective-permute-done | bytes 262176 | tf_op jit(solution)/shard_map/ppermute | solution.py:131
  15.7 0.7 copy.10
  16.5 0.0 all-gather.3.cloned.1.call-update
  16.5 6.5 %copy.16 = bf16[256,32,256]{2,0,1:T(8,128)(2,1)} copy(bf16[256,32,256]{2,1,0:T(8,128)(2,1)} %param.5) | data formatting | bytes 8388608 | tf_op args[2]
  23.0 1.2 collective-permute-start.1
  24.2 18.7 %copy.15 = bf16[256,32,1024]{2,0,1:T(8,128)(2,1)} copy(bf16[256,32,1024]{2,1,0:T(8,128)(2,1)} %param.4) | data formatting | bytes 33554432 | tf_op args[1]
  43.0 17.6 %all-gather.5.cloned.1.call-done.w_ref = bf16[1024,2048]{1,0:T(8,128)(2,1)} async-done(((bf16[64,2048]{1,0:T(8,128)(2,1)}), bf16[1024,2048]{1,0:T(8,128)(2,1)}) %all-gather.5.cloned.1.call-update) | async-done | bytes 4194320 | tf_op jit(solution)/shard_map/all_gather | solution.py:141
  60.5 49.5 %shard_map.37.rest_0_ = f32[2048,256]{1,0:T(8,128)} custom-call(bf16[32,256,1024]{2,1,0:T(8,128)(2,1)} %bitcast.19, bf16[1024,2048]{1,0:T(8,128)(2,1)} %all-gather.5.cloned.1.call-done.w_ref, bf16[32,256,256]{2,1,0:T(8,128)(2,1)} %bitcast.16.t_ref), custom_call_target="tpu_custom_call" | custom-call | flops 42949672960 | bytes 25165824 | tf_op jit(solution)/shard_map/pallas_call | solution.py:59
  110.0 3.8 %collective-permute-done.1.t_ref = bf16[32,256,256]{2,1,0:T(8,128)(2,1)} collective-permute-done((bf16[32,256,256]{2,1,0:T(8,128)(2,1)}, bf16[32,256,256]{2,1,0:T(8,128)(2,1)}, u32[]{:S(2)}, u32[]{:S(2)}) %collective-permute-start.1) | collective-permute-done | bytes 4194336 | tf_op jit(solution)/shard_map/ppermute | solution.py:131
  113.8 0.0 all-gather.3.cloned.1.call-done.w_ref
  113.9 50.0 %shard_map.38 = bf16[256,2048]{1,0:T(8,128)(2,1)} custom-call(bf16[32,256,1024]{2,1,0:T(8,128)(2,1)} %bitcast.20, bf16[1024,2048]{1,0:T(8,128)(2,1)} %all-gather.3.cloned.1.call-done.w_ref, bf16[32,256,256]{2,1,0:T(8,128)(2,1)} %collective-permute-done.1.t_ref, f32[2048,256]{1,0:T(8,128)} %shard_map.37.rest_0_), custom_call_target="tpu_custom_call" | custom-call | flops 42949672960 | bytes 25165824 | tf_op jit(solution)/shard_map/pallas_call | solution.py:59
  163.8 31.5 %shard_map.39 = f32[16,2048]{1,0:T(8,128)} custom-call(bf16[16,16,2048]{2,1,0:T(8,128)(2,1)} %bitcast.21), custom_call_target="tpu_custom_call" | custom-call | tf_op jit(solution)/shard_map/pallas_call | solution.py:105
  195.4 1.6 copy.17
Async XLA Ops:
  6.5 54.0 %all-gather.5.cloned.1.call-start = ((), (), s32[]{:S(2)}) async-start(), calls=%async_computation.1 | async-start | bytes 4456448 | tf_op jit(solution)/shard_map/all_gather | solution.py:141
  8.2 105.6 %all-gather.3.cloned.1.call-start = ((), (), s32[]{:S(2)}) async-start(), calls=%async_computation | async-start | bytes 4456448 | tf_op jit(solution)/shard_map/all_gather | solution.py:141
  8.3 7.5 %collective-permute-start = (bf16[64,8,256]{2,0,1:T(8,128)(2,1)}, bf16[64,8,256]{2,0,1:T(8,128)(2,1)S(1)}, u32[]{:S(2)}, u32[]{:S(2)}) collective-permute-start(bf16[64,8,256]{2,0,1:T(8,128)(2,1)} %bitcast.26), channel_id=1, source_target_pairs={{0,16},{16,0},{1,17},{17,1},{2,18},{18,2},{3,19},{19,3},{4,20},{20... | collective-permute-start | bytes 786440 | tf_op jit(solution)/shard_map/ppermute | solution.py:131
  23.0 90.8 %collective-permute-start.1 = (bf16[32,256,256]{2,1,0:T(8,128)(2,1)}, bf16[32,256,256]{2,1,0:T(8,128)(2,1)}, u32[]{:S(2)}, u32[]{:S(2)}) collective-permute-start(bf16[32,256,256]{2,1,0:T(8,128)(2,1)} %bitcast.16.t_ref), channel_id=1, source_target_pairs={{0,16},{16,0},{1,17},{17,1},{2,18},{18,2},{3,19},{19,3},{4,20},{20... | collective-permute-start | bytes 12582920 | tf_op jit(solution)/shard_map/ppermute | solution.py:131
Sparse Core Ops, SparseCore 0:
  9.5 51.0 all-gather.4
  62.7 48.8 all-gather.2

commit v3 on v2

--- a/solution.py
+++ b/solution.py
@@ -35,7 +35,7 @@
 
     @pl.when(step == pl.num_programs(0) - 1)
     def _():
-        out_ref[...] = acc[...].T.astype(out_ref.dtype) if last else acc[...]
+        out_ref[...] = acc[...].T if last else acc[...]
 
 
 def ladder_call(p_t, w, t, prev, last):
@@ -58,7 +58,7 @@
     flops = 2 * d * b * width * (q + n)
     return pl.pallas_call(
         functools.partial(ladder_kernel, c, last, prev is None),
-        out_shape=jax.ShapeDtypeStruct(out, jnp.bfloat16 if last else jnp.float32),
+        out_shape=jax.ShapeDtypeStruct(out, jnp.float32),
         grid=(d // d_block,),
         in_specs=in_specs,
         out_specs=whole(out),
@@ -71,46 +71,85 @@
     )(*args)
 
 
-def scatter_kernel(cols, x_ref, out_ref, held, send_sem, recv_sem):
+def scatter_kernel(cols, pair, x_ref, out_ref, near, sums, far, near_send, near_recv, far_send, far_recv):
     me = lax.axis_index("col")
+    pairs = cols // pair
+    core, mine = lax.rem(me, pair), lax.div(me, pair)
+    partner = mine * pair + lax.rem(core + 1, pair)
+
+    def place(s):
+        return lax.rem(mine + s, pairs) * pair
+
     barrier = pltpu.get_barrier_semaphore()
-    for s in range(1, cols):
-        pl.semaphore_signal(barrier, inc=1, device_id={"col": lax.rem(me + s, cols)}, device_id_type=MESH)
-    pl.semaphore_wait(barrier, cols - 1)
-    copies = []
-    for s in range(1, cols):
-        to = lax.rem(me + s, cols)
+    others = [place(s) + core for s in range(1, pairs)] + [partner] * (pair - 1)
+    for other in others:
+        pl.semaphore_signal(barrier, inc=1, device_id={"col": other}, device_id_type=MESH)
+    pl.semaphore_wait(barrier, len(others))
+
+    order = [*range(1, pairs), 0]
+    near_copies = {}
+    if pair == 2:
+        for s in order:
+            near_copies[s] = pltpu.make_async_remote_copy(
+                src_ref=x_ref.at[place(s) + lax.rem(core + 1, pair)],
+                dst_ref=near.at[s],
+                send_sem=near_send.at[s],
+                recv_sem=near_recv.at[s],
+                device_id={"col": partner},
+                device_id_type=MESH,
+            )
+            near_copies[s].start()
+
+    def pair_sum(s):
+        own = x_ref[place(s) + core]
+        if pair == 1:
+            return own
+        near_copies[s].wait_recv()
+        return own + near[s]
+
+    far_copies = []
+    for s in range(1, pairs):
+        sums[s - 1] = pair_sum(s).astype(sums.dtype)
         copy = pltpu.make_async_remote_copy(
-            src_ref=x_ref.at[to],
-            dst_ref=held.at[s - 1],
-            send_sem=send_sem.at[s - 1],
-            recv_sem=recv_sem.at[s - 1],
-            device_id={"col": to},
+            src_ref=sums.at[s - 1],
+            dst_ref=far.at[s - 1],
+            send_sem=far_send.at[s - 1],
+            recv_sem=far_recv.at[s - 1],
+            device_id={"col": place(s) + core},
             device_id_type=MESH,
         )
         copy.start()
-        copies.append(copy)
-    total = x_ref[me].astype(jnp.float32)
-    for s, copy in enumerate(copies):
+        far_copies.append(copy)
+    total = pair_sum(0)
+    for s, copy in enumerate(far_copies):
         copy.wait_recv()
-        total = total + held[s].astype(jnp.float32)
+        total = total + far[s].astype(jnp.float32)
     out_ref[...] = total
-    for copy in copies:
+    for copy in far_copies:
+        copy.wait_send()
+    for copy in near_copies.values():
         copy.wait_send()
 
 
 def scatter_call(x, cols):
     n, width = x.shape
     piece = (n // cols, width)
+    pair = 2 if cols % 2 == 0 else 1
+    pairs = cols // pair
+    far = max(pairs - 1, 1)
     return pl.pallas_call(
-        functools.partial(scatter_kernel, cols),
+        functools.partial(scatter_kernel, cols, pair),
         out_shape=jax.ShapeDtypeStruct(piece, jnp.float32),
         in_specs=[pl.BlockSpec(memory_space=pltpu.VMEM)],
         out_specs=pl.BlockSpec(memory_space=pltpu.VMEM),
         scratch_shapes=[
-            pltpu.VMEM((cols - 1, *piece), x.dtype),
-            pltpu.SemaphoreType.DMA((cols - 1,)),
-            pltpu.SemaphoreType.DMA((cols - 1,)),
+            pltpu.VMEM((pairs, *piece), jnp.float32),
+            pltpu.VMEM((far, *piece), jnp.bfloat16),
+            pltpu.VMEM((far, *piece), jnp.bfloat16),
+            pltpu.SemaphoreType.DMA((pairs,)),
+            pltpu.SemaphoreType.DMA((pairs,)),
+            pltpu.SemaphoreType.DMA((far,)),
+            pltpu.SemaphoreType.DMA((far,)),
         ],
         compiler_params=pltpu.CompilerParams(collective_id=0, has_side_effects=True),
     )(x.reshape(cols, *piece))
@@ -128,7 +167,8 @@
         blocks = [(w_own, t_own)]
         for shift in range(1, row_count):
             pairs = [(i, (i + shift) % row_count) for i in range(row_count)]
-            blocks.append((lax.ppermute(w_own, "row", pairs), lax.ppermute(t_own, "row", pairs)))
+            w_far, t_held = lax.optimization_barrier((lax.ppermute(w_own, "row", pairs), t_own))
+            blocks.append((w_far, lax.ppermute(t_held, "row", pairs)))
     else:
         blocks = [(
             lax.all_gather(w_own, "row", axis=2, tiled=True),

time: 204 us -> 190 us (0.931)
  Pallas kernels: 131 us -> 119 us
    pallas_call x1, Pallas kernels: 31.5 us -> 19.2 us  [scatter_call(): pl.pallas_call(functools.partial(scatter_kernel, cols, pair), out_shape=j...]
    all_gather x2, waiting for transfers between devices: 17.6 us -> 25.6 us  [local(): w = lax.all_gather(w.reshape(q_own, -1), 'col', axis=0, tiled=True)]
    ppermute x1, waiting for transfers between devices: 6.19 us -> 0.01 us  [local(): lax.ppermute(w_own, 'row', pairs)]
    ppermute x1, waiting for transfers between devices: 3.83 us -> 0.01 us  [local(): blocks.append((w_far, lax.ppermute(t_held, 'row', pairs)))]
  transfers between devices with their start and end apart: 4 -> 4, of which waited for: 3 -> 2; matrix products, arithmetic and copies ran while one was open for 13% -> 14% of each run, Pallas kernels for 24% -> 26%
where the time goes in v3:
time: 190 us
  Pallas kernels  119 us (63%)
  local copies, waits for them, and re-layouts  29.2 us (15%)
  waiting for transfers between devices  25.7 us (14%)
  between operations  13.4 us (7%)
  starting transfers between devices  2.3 us (1%)
    pallas_call x2, Pallas kernels, ladder_call(): pl.pallas_call(functools.partial(ladder_kernel, c, last, prev is None), o...  100 us
    all_gather x2, waiting for transfers between devices, local(): w = lax.all_gather(w.reshape(q_own, -1), 'col', axis=0, tiled=True)  25.6 us
    unnamed x2, local copies, waits for them, and re-layouts  25.2 us
    pallas_call x1, Pallas kernels, scatter_call(): pl.pallas_call(functools.partial(scatter_kernel, cols, pair), out_shape=j...  19.2 us
  transfers between devices with their start and end apart: 4, of which 2 were waited for; matrix products, arithmetic and copies ran while one was open for 14% of the time, Pallas kernels for 26%

profile of v3, /device:TPU:13, one launch (start us, length us, event | category | flops | bytes accessed | tf_op | source)
XLA Modules:
  0.0 189.9 jit_solution(9808752717471747900)
XLA Ops:
  6.5 0.0 all-gather.5.cloned.1.call-start
  6.5 1.7 copy.11
  8.2 0.0 all-gather.5.cloned.1.call-update
  8.2 0.0 all-gather.3.cloned.1.call-start
  8.3 1.3 collective-permute-start
  9.6 6.5 %copy.16 = bf16[256,32,256]{2,0,1:T(8,128)(2,1)} copy(bf16[256,32,256]{2,1,0:T(8,128)(2,1)} %param.5) | data formatting | bytes 8388608 | tf_op args[2]
  16.0 0.0 collective-permute-done
  16.0 0.7 copy.10
  16.8 0.0 all-gather.3.cloned.1.call-update
  16.8 1.0 collective-permute-start.1
  17.8 18.8 %copy.15 = bf16[256,32,1024]{2,0,1:T(8,128)(2,1)} copy(bf16[256,32,1024]{2,1,0:T(8,128)(2,1)} %param.4) | data formatting | bytes 33554432 | tf_op args[1]
  36.5 24.0 %all-gather.5.cloned.1.call-done.w_ref = bf16[1024,2048]{1,0:T(8,128)(2,1)} async-done(((bf16[64,2048]{1,0:T(8,128)(2,1)}), bf16[1024,2048]{1,0:T(8,128)(2,1)}) %all-gather.5.cloned.1.call-update) | async-done | bytes 4194320 | tf_op jit(solution)/shard_map/all_gather | solution.py:181
  60.5 49.5 %shard_map.37.rest_0_ = f32[2048,256]{1,0:T(8,128)} custom-call(bf16[32,256,1024]{2,1,0:T(8,128)(2,1)} %bitcast.19, bf16[1024,2048]{1,0:T(8,128)(2,1)} %all-gather.5.cloned.1.call-done.w_ref, bf16[32,256,256]{2,1,0:T(8,128)(2,1)} %bitcast.22), custom_call_target="tpu_custom_call" | custom-call | flops 42949672960 | bytes 25165824 | tf_op jit(solution)/shard_map/pallas_call | solution.py:59
  110.0 0.0 collective-permute-done.1.t_ref
  110.0 1.6 all-gather.3.cloned.1.call-done.w_ref
  111.6 50.6 %shard_map.38 = f32[256,2048]{1,0:T(8,128)} custom-call(bf16[32,256,1024]{2,1,0:T(8,128)(2,1)} %bitcast.20, bf16[1024,2048]{1,0:T(8,128)(2,1)} %all-gather.3.cloned.1.call-done.w_ref, bf16[32,256,256]{2,1,0:T(8,128)(2,1)} %collective-permute-done.1.t_ref, f32[2048,256]{1,0:T(8,128)} %shard_map.37.rest_0_), custom_call_target="tpu_custom_call" | custom-call | flops 42949672960 | bytes 25165824 | tf_op jit(solution)/shard_map/pallas_call | solution.py:59
  162.2 19.2 %shard_map.39 = f32[16,2048]{1,0:T(8,128)} custom-call(f32[16,16,2048]{2,1,0:T(8,128)} %bitcast.23), custom_call_target="tpu_custom_call" | custom-call | tf_op jit(solution)/shard_map/pallas_call | solution.py:140
  181.5 1.6 copy.17
Async XLA Ops:
  6.5 54.0 %all-gather.5.cloned.1.call-start = ((), (), s32[]{:S(2)}) async-start(), calls=%async_computation.1 | async-start | bytes 4456448 | tf_op jit(solution)/shard_map/all_gather | solution.py:181
  8.2 103.4 %all-gather.3.cloned.1.call-start = ((), (), s32[]{:S(2)}) async-start(), calls=%async_computation | async-start | bytes 4456448 | tf_op jit(solution)/shard_map/all_gather | solution.py:181
  8.3 7.8 %collective-permute-start = (bf16[64,8,256]{2,0,1:T(8,128)(2,1)}, bf16[64,8,256]{2,0,1:T(8,128)(2,1)S(1)}, u32[]{:S(2)}, u32[]{:S(2)}) collective-permute-start(bf16[64,8,256]{2,0,1:T(8,128)(2,1)} %bitcast.28), channel_id=1, source_target_pairs={{0,16},{16,0},{1,17},{17,1},{2,18},{18,2},{3,19},{19,3},{4,20},{20... | collective-permute-start | bytes 786440 | tf_op jit(solution)/shard_map/ppermute | solution.py:170
  16.8 93.2 %collective-permute-start.1 = (bf16[32,256,256]{2,1,0:T(8,128)(2,1)}, bf16[32,256,256]{2,1,0:T(8,128)(2,1)}, u32[]{:S(2)}, u32[]{:S(2)}) collective-permute-start(bf16[32,256,256]{2,1,0:T(8,128)(2,1)} %bitcast.21), channel_id=1, source_target_pairs={{0,16},{16,0},{1,17},{17,1},{2,18},{18,2},{3,19},{19,3},{4,20},{20... | collective-permute-start | bytes 12582920 | tf_op jit(solution)/shard_map/ppermute | solution.py:171
Sparse Core Ops, SparseCore 0:
  9.5 51.0 all-gather.4
  62.7 48.8 all-gather.2

commit v4 on v3

--- a/solution.py
+++ b/solution.py
@@ -124,14 +124,16 @@
     for s, copy in enumerate(far_copies):
         copy.wait_recv()
         total = total + far[s].astype(jnp.float32)
-    out_ref[...] = total
+    b = out_ref.shape[2]
+    for a in range(out_ref.shape[0]):
+        out_ref[a] = total[:, a * b:(a + 1) * b]
     for copy in far_copies:
         copy.wait_send()
     for copy in near_copies.values():
         copy.wait_send()
 
 
-def scatter_call(x, cols):
+def scatter_call(x, cols, width_a):
     n, width = x.shape
     piece = (n // cols, width)
     pair = 2 if cols % 2 == 0 else 1
@@ -139,7 +141,7 @@
     far = max(pairs - 1, 1)
     return pl.pallas_call(
         functools.partial(scatter_kernel, cols, pair),
-        out_shape=jax.ShapeDtypeStruct(piece, jnp.float32),
+        out_shape=jax.ShapeDtypeStruct((width_a, n // cols, width // width_a), jnp.float32),
         in_specs=[pl.BlockSpec(memory_space=pltpu.VMEM)],
         out_specs=pl.BlockSpec(memory_space=pltpu.VMEM),
         scratch_shapes=[
@@ -157,7 +159,6 @@
 
 def local(row_count, col_count, chol_window, pair_vectors, amplitudes):
     c, width_a, q_own = chol_window.shape
-    b = pair_vectors.shape[0]
 
     w_own = chol_window.transpose(2, 1, 0)
     t_own = amplitudes.transpose(1, 0, 2)
@@ -180,8 +181,7 @@
     for index, (w, t) in enumerate(blocks):
         w = lax.all_gather(w.reshape(q_own, -1), "col", axis=0, tiled=True)
         total = ladder_call(p_t, w, t, total, index == len(blocks) - 1)
-    out = scatter_call(total, col_count)
-    return out.reshape(out.shape[0], width_a, b).transpose(1, 0, 2)
+    return scatter_call(total, col_count, width_a)
 
 
 def solution(mesh):

time: 190 us -> 190 us (level)
    unnamed x2 -> x3, local copies, waits for them, and re-layouts: 25.2 us -> 26.8 us
where the time goes in v4:
time: 190 us
  Pallas kernels  119 us (63%)
  local copies, waits for them, and re-layouts  29.2 us (15%)
  waiting for transfers between devices  25.7 us (14%)
  between operations  13.4 us (7%)
  starting transfers between devices  2.3 us (1%)
    pallas_call x2, Pallas kernels, ladder_call(): pl.pallas_call(functools.partial(ladder_kernel, c, last, prev is None), o...  100 us
    unnamed x3, local copies, waits for them, and re-layouts  26.8 us
    all_gather x2, waiting for transfers between devices, local(): w = lax.all_gather(w.reshape(q_own, -1), 'col', axis=0, tiled=True)  25.6 us
    pallas_call x1, Pallas kernels, scatter_call(): pl.pallas_call(functools.partial(scatter_kernel, cols, pair), out_shape=j...  19.2 us
  transfers between devices with their start and end apart: 4, of which 2 were waited for; matrix products, arithmetic and copies ran while one was open for 14% of the time, Pallas kernels for 26%

profile of v4, /device:TPU:13, one launch (start us, length us, event | category | flops | bytes accessed | tf_op | source)
XLA Modules:
  0.0 189.9 jit_solution(12214302621125588321)
XLA Ops:
  6.5 0.0 all-gather.5.cloned.1.call-start
  6.5 1.7 copy.9
  8.2 0.0 all-gather.5.cloned.1.call-update
  8.2 0.0 all-gather.3.cloned.1.call-start
  8.3 1.3 collective-permute-start
  9.6 6.5 %copy.13 = bf16[256,32,256]{2,0,1:T(8,128)(2,1)} copy(bf16[256,32,256]{2,1,0:T(8,128)(2,1)} %param.5) | data formatting | bytes 8388608 | tf_op args[2]
  16.0 0.0 collective-permute-done
  16.0 0.7 copy.8
  16.8 0.0 all-gather.3.cloned.1.call-update
  16.8 1.0 collective-permute-start.1
  17.8 18.8 %copy.12 = bf16[256,32,1024]{2,0,1:T(8,128)(2,1)} copy(bf16[256,32,1024]{2,1,0:T(8,128)(2,1)} %param.4) | data formatting | bytes 33554432 | tf_op args[1]
  36.5 24.0 %all-gather.5.cloned.1.call-done.w_ref = bf16[1024,2048]{1,0:T(8,128)(2,1)} async-done(((bf16[64,2048]{1,0:T(8,128)(2,1)}), bf16[1024,2048]{1,0:T(8,128)(2,1)}) %all-gather.5.cloned.1.call-update) | async-done | bytes 4194320 | tf_op jit(solution)/shard_map/all_gather | solution.py:182
  60.5 49.5 %shard_map.37.rest_0_ = f32[2048,256]{1,0:T(8,128)} custom-call(bf16[32,256,1024]{2,1,0:T(8,128)(2,1)} %bitcast.12, bf16[1024,2048]{1,0:T(8,128)(2,1)} %all-gather.5.cloned.1.call-done.w_ref, bf16[32,256,256]{2,1,0:T(8,128)(2,1)} %bitcast.15), custom_call_target="tpu_custom_call" | custom-call | flops 42949672960 | bytes 25165824 | tf_op jit(solution)/shard_map/pallas_call | solution.py:59
  110.0 0.0 collective-permute-done.1.t_ref
  110.0 1.6 all-gather.3.cloned.1.call-done.w_ref
  111.6 50.6 %shard_map.38 = f32[256,2048]{1,0:T(8,128)} custom-call(bf16[32,256,1024]{2,1,0:T(8,128)(2,1)} %bitcast.13, bf16[1024,2048]{1,0:T(8,128)(2,1)} %all-gather.3.cloned.1.call-done.w_ref, bf16[32,256,256]{2,1,0:T(8,128)(2,1)} %collective-permute-done.1.t_ref, f32[2048,256]{1,0:T(8,128)} %shard_map.37.rest_0_), custom_call_target="tpu_custom_call" | custom-call | flops 42949672960 | bytes 25165824 | tf_op jit(solution)/shard_map/pallas_call | solution.py:59
  162.2 19.2 %shard_map.39 = f32[8,16,256]{2,1,0:T(8,128)} custom-call(f32[16,16,2048]{2,1,0:T(8,128)} %bitcast.16), custom_call_target="tpu_custom_call" | custom-call | tf_op jit(solution)/shard_map/pallas_call | solution.py:142
  181.5 1.6 copy.15
Async XLA Ops:
  6.5 54.0 %all-gather.5.cloned.1.call-start = ((), (), s32[]{:S(2)}) async-start(), calls=%async_computation.1 | async-start | bytes 4456448 | tf_op jit(solution)/shard_map/all_gather | solution.py:182
  8.2 103.4 %all-gather.3.cloned.1.call-start = ((), (), s32[]{:S(2)}) async-start(), calls=%async_computation | async-start | bytes 4456448 | tf_op jit(solution)/shard_map/all_gather | solution.py:182
  8.3 7.8 %collective-permute-start = (bf16[64,8,256]{2,0,1:T(8,128)(2,1)}, bf16[64,8,256]{2,0,1:T(8,128)(2,1)S(1)}, u32[]{:S(2)}, u32[]{:S(2)}) collective-permute-start(bf16[64,8,256]{2,0,1:T(8,128)(2,1)} %bitcast.20), channel_id=1, source_target_pairs={{0,16},{16,0},{1,17},{17,1},{2,18},{18,2},{3,19},{19,3},{4,20},{20... | collective-permute-start | bytes 786440 | tf_op jit(solution)/shard_map/ppermute | solution.py:171
  16.8 93.2 %collective-permute-start.1 = (bf16[32,256,256]{2,1,0:T(8,128)(2,1)}, bf16[32,256,256]{2,1,0:T(8,128)(2,1)}, u32[]{:S(2)}, u32[]{:S(2)}) collective-permute-start(bf16[32,256,256]{2,1,0:T(8,128)(2,1)} %bitcast.14), channel_id=1, source_target_pairs={{0,16},{16,0},{1,17},{17,1},{2,18},{18,2},{3,19},{19,3},{4,20},{20... | collective-permute-start | bytes 12582920 | tf_op jit(solution)/shard_map/ppermute | solution.py:172
Sparse Core Ops, SparseCore 0:
  9.5 51.0 all-gather.4
  62.7 48.8 all-gather.2
